TPU v7x, 512 devices: a whole 4x8x8 slice. The times are simulated.
512 devices in a mesh: tok: 64 (over z, y_hi, x), feat: 8 (over y_lo, core).
Axes of the slice: x: 4, y: 8 (y_hi: 2, y_lo: 4; y = y_hi * 4 + y_lo), z: 8, core: 2. Of those that a mesh axis runs over, the one named last changes fastest.
Arguments:
- activations: bfloat16 [131072, 8192], P('tok', 'feat')
- labels: int32 [131072], P('tok'), may hold values from 0 to 7, as said below
Outputs:
- cov_panel: float32 [1024, 8192], P('tok', 'feat')
- cross_cov: float32 [8, 8192], P(None, 'feat')
Inputs may be any that keep to these rules, and one draw needn't show every extreme that they name: `labels`: each token's class.
All inputs are finite; a program needn't handle non-finite values.
Results may differ from a plain program's by a relative error of at most 0.0017.
Values may be sent and summed in bfloat16 or wider, within the bound.
A program may use at most 64 MiB of HBM per device.

v0:
```python
import jax
import jax.numpy as jnp
from jax import lax
from jax.sharding import PartitionSpec as P

CLASSES = 8
PANEL = 128


def tokens_product(left, right):
    return lax.dot_general(
        left, right, (((0,), (0,)), ((), ())), preferred_element_type=jnp.float32
    )


def body(activations, labels):
    tok_rows = activations.shape[0]
    total = tok_rows * lax.axis_size("tok")
    column_total = lax.psum(jnp.sum(activations, axis=0, dtype=jnp.float32), "tok")
    mean = column_total / total
    centered = (activations.astype(jnp.float32) - mean).astype(jnp.bfloat16)
    onehot = (labels[:, None] == jnp.arange(CLASSES, dtype=jnp.int32)[None, :]).astype(jnp.bfloat16)
    class_part = tokens_product(onehot, centered)
    class_total = lax.psum(class_part, "tok")
    cross_cov = class_total / total
    outgoing = centered[:, :PANEL]
    panel = lax.all_gather(outgoing, "feat", axis=1, tiled=True)
    summed = lax.psum_scatter(
        tokens_product(panel, centered), "tok", scatter_dimension=0, tiled=True
    )
    cov_panel = summed / (total - 1)
    return (cov_panel, cross_cov)


def solution(mesh):
    in_specs = (P("tok", "feat"), P("tok"))
    out_specs = (P("tok", "feat"), P(None, "feat"))
    return jax.shard_map(body, mesh=mesh, in_specs=in_specs, out_specs=out_specs, check_vma=False)
```

profile of v0, /device:TPU:8, one launch (start us, length us, event | category | flops | bytes accessed | tf_op | source)
XLA Modules:
  0.0 762.9 jit_solution(16792029753697239541)
XLA Ops:
  7.2 0.0 all-gather.2.cloned.1.call-start
  7.2 2.9 convert_reduce_fusion
  10.1 230.5 %psum.14 = f32[1024]{0:T(1024)S(1)} all-reduce(f32[1024]{0:T(1024)S(1)} %convert_reduce_fusion), channel_id=1, replica_groups=mesh['tok'=64,'feat'=8] {'tok'}, use_global_device_ids=true, to_apply=%region_1.0 | all-reduce | flops 1024 | bytes 8192 | tf_op jit(solution)/shard_map/psum | solution.py:19
  240.5 3.3 fusion
  243.9 0.0 copy-start
  243.9 1.9 copy-done
  245.8 0.9 slice.4
  246.7 0.0 all-gather.2.cloned.1.call-update
  246.8 0.0 reduce-scatter.2.cloned.1.call-start
  246.8 45.1 %all-gather.2.cloned.1.call-done = bf16[2048,1024]{1,0:T(8,128)(2,1)} async-done(((bf16[2048,128]{1,0:T(8,128)(2,1)}), bf16[2048,1024]{1,0:T(8,128)(2,1)}) %all-gather.2.cloned.1.call-update) | async-done | bytes 4194320 | tf_op jit(solution)/shard_map/all_gather | solution.py:27
  291.9 10.0 %fusion.3 = f32[1024,1024]{1,0:T(8,128)} fusion(bf16[2048,1024]{1,0:T(8,128)(2,1)} %all-gather.2.cloned.1.call-done, bf16[2048,1024]{1,0:T(8,128)(2,1)} %copy-done), kind=kOutput, calls=%fused_computation.9 | convolution fusion | flops 4294967296 | bytes 12582912 | tf_op jit(solution)/shard_map/dot_general | solution.py:11
  301.9 0.0 copy-start.1
  301.9 0.0 reduce-scatter.2.cloned.1.call-update
  301.9 0.7 copy-done.1
  302.6 3.1 fusion.1
  305.7 437.9 %psum.15 = f32[8,1024]{1,0:T(8,128)S(1)} all-reduce(f32[8,1024]{1,0:T(8,128)S(1)} %fusion.1), channel_id=1, replica_groups=mesh['tok'=64,'feat'=8] {'tok'}, use_global_device_ids=true, to_apply=%region_3.0 | all-reduce | flops 8192 | bytes 65536 | tf_op jit(solution)/shard_map/psum | solution.py:24
  743.7 0.6 broadcast_multiply_fusion.1
  744.3 10.3 %reduce-scatter.2.cloned.1.call-done = f32[16,1024]{1,0:T(8,128)} async-done(((f32[1024,1024]{1,0:T(8,128)}), f32[16,1024]{1,0:T(8,128)}) %reduce-scatter.2.cloned.1.call-update) | async-done | bytes 65552 | tf_op jit(solution)/shard_map/reduce_scatter | solution.py:28
  754.6 1.5 broadcast_multiply_fusion
  (1 shorter events, 0.0 us)
Async XLA Ops:
  7.2 284.7 %all-gather.2.cloned.1.call-start = ((), (), s32[]{:S(2)}) async-start(), calls=%async_computation.1 | async-start | bytes 4718592 | tf_op jit(solution)/shard_map/all_gather | solution.py:27
  243.9 1.9 copy-start
  246.8 507.8 %reduce-scatter.2.cloned.1.call-start = ((), (), s32[]{:S(2)}) async-start(), calls=%async_computation.2 | async-start | bytes 4259840 | tf_op jit(solution)/shard_map/reduce_scatter | solution.py:28
  301.9 0.7 copy-start.1
Sparse Core Ops, SparseCore 0:
  246.9 44.9 all-gather.1
  302.0 452.4 reduce-scatter.1
where the time goes:
time: 763 us
  blocking collectives  668 us (88%)
  waiting for transfers between devices  55.4 us (7%)
  between operations  14.1 us (2%)
  matrix products  13.1 us (2%)
  other arithmetic  8.3 us (1%)
    psum x1, blocking collectives, body(): class_total = lax.psum(class_part, 'tok')  438 us
    psum x1, blocking collectives, body(): lax.psum(jnp.sum(activations, axis=0, dtype=jnp.float32), 'tok')  230 us
    all_gather x1, waiting for transfers between devices, body(): panel = lax.all_gather(outgoing, 'feat', axis=1, tiled=True)  45.1 us
  transfers between devices with their start and end apart: 2, of which 2 were waited for; matrix products, arithmetic and copies ran while one was open for 0% of the time, Pallas kernels for 0%

commit v1 on v0

v1 whole, which is shorter than its diff:
```python
import functools

import jax
import jax.numpy as jnp
from jax import lax
from jax.experimental import pallas as pl
from jax.experimental.pallas import tpu as pltpu
from jax.sharding import PartitionSpec as P

CLASSES = 8
PANEL = 128
NZ, NYH, NX = 8, 2, 4
NY, NC = 4, 2
NF = NY * NC
Q = 4
ROWS = PANEL // Q
MESH = pl.DeviceIdType.MESH
F32 = jnp.float32
BF16 = jnp.bfloat16


def chunk_column(row):
    q0 = (row >> 5) & 1
    q1 = (row >> 6) & 1
    x = (row >> 3) & 3
    return 16 * (q0 * 4 + x) + 8 * q1 + (row & 7)


def to_tile(row_value, ref):
    for i in range(8):
        ref[i : i + 1, :] = row_value[:, 128 * i : 128 * (i + 1)]


def kernel(
    act_hbm, labels_ref, cov_ref, cross_ref,
    abuf, cbuf, pan, lhs, accf, xs, xr, zsum, zs, zr, ykeep, ysend, yr,
    mz, mx, my, mf, mrow, mcol, crs, crr, cx, cy, cg,
    load_sem, ag_r, ag_right, ag_left, ag_part,
    x_s, x_r, z_s, z_r, y_s, y_r,
    mz_s, mz_r, mx_s, mx_r, my_s, my_r, mf_s, mf_r,
    cr_s, cr_r, cx_s, cx_r, cy_s, cy_r, cg_s, cg_r,
):
    tokens, width = abuf.shape
    tok = lax.axis_index("tok")
    feat = lax.axis_index("feat")
    z = tok // (NYH * NX)
    yh = (tok // NX) % NYH
    x = tok % NX
    y = feat // NC
    c = feat % NC
    total = tokens * NZ * NYH * NX

    def dev(zz=None, hh=None, xx=None, ff=None):
        zz = z if zz is None else zz
        hh = yh if hh is None else hh
        xx = x if xx is None else xx
        ff = feat if ff is None else ff
        return {"tok": (zz * NYH + hh) * NX + xx, "feat": ff}

    def remote(src, dst, send, recv, device):
        return pltpu.make_async_remote_copy(
            src_ref=src, dst_ref=dst, send_sem=send, recv_sem=recv,
            device_id=device, device_id_type=MESH,
        )

    first = pltpu.make_async_copy(
        act_hbm.at[:, pl.ds(0, PANEL)], abuf.at[:, pl.ds(0, PANEL)], load_sem.at[0])
    rest = pltpu.make_async_copy(
        act_hbm.at[:, pl.ds(PANEL, width - PANEL)],
        abuf.at[:, pl.ds(PANEL, width - PANEL)], load_sem.at[1])
    first.start()
    rest.start()

    barrier = pltpu.get_barrier_semaphore()
    for d in range(1, NF):
        pl.semaphore_signal(barrier, inc=1, device_id=dev(ff=(feat + d) % NF), device_id_type=MESH)
    for d in range(1, NZ):
        pl.semaphore_signal(barrier, inc=1, device_id=dev(zz=(z + d) % NZ), device_id_type=MESH)
    for d in range(1, NX):
        pl.semaphore_signal(barrier, inc=1, device_id=dev(xx=(x + d) % NX), device_id_type=MESH)
    pl.semaphore_signal(barrier, inc=1, device_id=dev(hh=1 - yh), device_id_type=MESH)

    first.wait()
    rows = lax.broadcasted_iota(jnp.int32, (PANEL, PANEL), 0)
    lanes = lax.broadcasted_iota(jnp.int32, (PANEL, PANEL), 1)
    pick = lanes == chunk_column(rows)
    select = jnp.where(pick, 1.0, 0.0).astype(BF16)
    for i in range(4):
        part = tokens // 4
        turned = lax.dot_general(
            select, abuf[i * part : (i + 1) * part, :PANEL],
            (((1,), (1,)), ((), ())), preferred_element_type=F32).astype(BF16)
        for q in range(Q):
            pan[q, feat, :, i * part : (i + 1) * part] = turned[q * ROWS : (q + 1) * ROWS, :]

    rest.wait()

    def add_rows(i, carry):
        block = abuf[pl.ds(pl.multiple_of(i * 64, 64), 64), :].astype(F32)
        return carry + jnp.sum(block.reshape(8, 8, width), axis=0)

    sums = lax.fori_loop(0, tokens // 64, add_rows, jnp.zeros((8, width), F32))
    to_tile(jnp.sum(sums, axis=0, keepdims=True), mz.at[z])

    pl.semaphore_wait(barrier, (NF - 1) + (NZ - 1) + (NX - 1) + 1)

    def panel_copy(q, f, device, send):
        return remote(pan.at[q, f], pan.at[q, f], send.at[q, f], ag_r.at[q, f], device)

    def go_right(q, f):
        return panel_copy(q, f, dev(ff=(feat + NC) % NF), ag_right)

    def go_left(q, f):
        return panel_copy(q, f, dev(ff=(feat + NF - NC) % NF), ag_left)

    def go_part(q, f):
        return panel_copy(q, f, dev(ff=y * NC + 1 - c), ag_part)

    def ag_own(q):
        @pl.when(y < NY - 1)
        def _():
            go_right(q, feat).start()

        @pl.when(y > 0)
        def _():
            go_left(q, feat).start()

        go_part(q, feat).start()

    def ag_recv(q):
        for k in range(1, NY):
            @pl.when(y >= k)
            def _():
                f = feat - NC * k
                go_part(q, f).wait_recv()

                @pl.when(y < NY - 1)
                def _():
                    go_right(q, f).start()

                go_part(q, f).start()

            @pl.when(y + k < NY)
            def _():
                f = feat + NC * k
                go_part(q, f).wait_recv()

                @pl.when(y > 0)
                def _():
                    go_left(q, f).start()

                go_part(q, f).start()

        for yy in range(NY):
            go_part(q, yy * NC + 1 - c).wait_recv()

    def ag_drain():
        for q in range(Q):
            for yy in range(NY):
                f = yy * NC + c

                @pl.when((y < NY - 1) & (y >= yy))
                def _():
                    go_right(q, f).wait_send()

                @pl.when((y > 0) & (y <= yy))
                def _():
                    go_left(q, f).wait_send()

                go_part(q, f).wait_send()

    def z_copy(buf, src, dst, send, recv, d):
        to = (z + d) % NZ
        return remote(src, dst, send.at[to], recv.at[z], dev(zz=to))

    def exchange_start(buf, own, n, send, recv, where):
        for d in range(1, n):
            to = (own + d) % n
            remote(buf.at[own], buf.at[own], send.at[to], recv.at[own], where(to)).start()

    def exchange_wait(buf, own, n, send, recv, where):
        for d in range(1, n):
            to = (own + d) % n
            remote(buf.at[own], buf.at[own], send.at[to], recv.at[own], where(to)).wait_send()
            remote(buf.at[to], buf.at[to], send.at[to], recv.at[to], where(to)).wait_recv()

    def at_z(to):
        return dev(zz=to)

    def at_x(to):
        return dev(xx=to)

    def at_h(to):
        return dev(hh=to)

    def at_f(to):
        return dev(ff=to)

    def slot_sum(buf, n):
        value = buf[0]
        for i in range(1, n):
            value = value + buf[i]
        return value

    def compute(q):
        for f in range(NF):
            block = pan[q, f].astype(F32) - mcol[f, q * ROWS : (q + 1) * ROWS, 0:1]
            lhs[f * ROWS : (f + 1) * ROWS, :] = block.astype(BF16)

        def columns(n, carry):
            at = pl.ds(pl.multiple_of(n * 256, 256), 256)
            acc = jnp.dot(lhs[...], cbuf[:, at], preferred_element_type=F32)
            acc = acc.reshape(NF, NX, 8, 256)
            for xx in range(NX):
                slab = acc[:, xx].reshape(NF * 8, 256)
                accf[q, xx, :, at] = slab
                xs[q, xx, :, at] = slab.astype(BF16)
            return carry

        lax.fori_loop(0, width // 256, columns, 0)
        for d in range(1, NX):
            x_copy(q, d).start()

    def x_copy(q, d):
        to = (x + d) % NX
        return remote(xs.at[q, to], xr.at[q, d - 1], x_s.at[q, d - 1], x_r.at[q, d - 1], dev(xx=to))

    def z_send(q, d):
        to = (z + d) % NZ
        return remote(zs.at[q, to], zr.at[q, d - 1], z_s.at[q, d - 1], z_r.at[q, d - 1], dev(zz=to))

    def zphase(q):
        for d in range(1, NX):
            x_copy(q, d).wait_recv()
        for f in range(NF):
            at = slice(f * 8, f * 8 + 8)
            value = accf[q, x, at, :]
            for d in range(NX - 1):
                value = value + xr[q, d, at, :].astype(F32)
            zsum[q, f] = value
            half = width // 2
            zs[q, f] = jnp.concatenate([value[:, :half], value[:, half:]], axis=0).astype(BF16)
        for d in range(1, NZ):
            z_send(q, d).start()

    def y_send(half):
        return remote(ysend.at[half], yr.at[half], y_s.at[half], y_r.at[half], dev(hh=1 - yh))

    def yphase(q):
        for d in range(1, NZ):
            z_send(q, d).wait_recv()
        parts = jnp.zeros((16, width // 2), F32)
        for d in range(NZ - 1):
            parts = parts + zr[q, d].astype(F32)
        value = zsum[q, z] + jnp.concatenate([parts[:8], parts[8:]], axis=1)
        half = q // 2

        @pl.when(yh == q % 2)
        def _():
            ykeep[half] = value

        @pl.when(yh != q % 2)
        def _():
            ysend[half] = value
            y_send(half).start()

    exchange_start(mz, z, NZ, mz_s, mz_r, at_z)
    ag_own(0)
    ag_own(1)
    exchange_wait(mz, z, NZ, mz_s, mz_r, at_z)
    mx[x] = slot_sum(mz, NZ)
    exchange_start(mx, x, NX, mx_s, mx_r, at_x)
    ag_recv(0)
    exchange_wait(mx, x, NX, mx_s, mx_r, at_x)
    my[yh] = slot_sum(mx, NX)
    exchange_start(my, yh, NYH, my_s, my_r, at_h)
    ag_own(2)
    exchange_wait(my, yh, NYH, my_s, my_r, at_h)
    mean = slot_sum(my, NYH) / total
    mf[feat] = mean
    exchange_start(mf, feat, NF, mf_s, mf_r, at_f)
    for i in range(8):
        mrow[:, 128 * i : 128 * (i + 1)] = mean[i : i + 1, :]

    def center(i, carry):
        at = pl.ds(pl.multiple_of(i * 64, 64), 64)
        cbuf[at, :] = (abuf[at, :].astype(F32) - mrow[...]).astype(BF16)
        return carry

    lax.fori_loop(0, tokens // 64, center, 0)
    ag_recv(1)
    ag_own(3)

    exchange_wait(mf, feat, NF, mf_s, mf_r, at_f)
    for f in range(NF):
        value = jnp.where(pick, mf[f, 0:1, :], 0.0)
        mcol[f] = jnp.broadcast_to(jnp.sum(value, axis=1, keepdims=True), (PANEL, PANEL))

    compute(0)
    compute(1)

    classes = lax.broadcasted_iota(jnp.int32, (16, tokens), 0)
    onehot = jnp.where(classes == labels_ref[...], 1.0, 0.0).astype(BF16)

    def class_columns(n, carry):
        at = pl.ds(pl.multiple_of(n * 256, 256), 256)
        part = jnp.dot(onehot, cbuf[:, at], preferred_element_type=F32)
        for k in range(CLASSES):
            for i in range(2):
                crs[k, pl.ds(2 * n + i, 1), :] = part[k : k + 1, 128 * i : 128 * (i + 1)]
        return carry

    lax.fori_loop(0, width // 256, class_columns, 0)
    crr[z] = crs[z]

    def class_copy(d):
        to = (z + d) % NZ
        return remote(crs.at[to], crr.at[z], cr_s.at[to], cr_r.at[z], at_z(to))

    def class_from(d):
        to = (z + d) % NZ
        return remote(crs.at[to], crr.at[to], cr_s.at[to], cr_r.at[to], at_z(to))

    for d in range(1, NZ):
        class_copy(d).start()

    zphase(0)
    ag_recv(2)
    compute(2)

    for d in range(1, NZ):
        class_copy(d).wait_send()
        class_from(d).wait_recv()
    cx[x] = slot_sum(crr, NZ)
    exchange_start(cx, x, NX, cx_s, cx_r, at_x)

    zphase(1)
    yphase(0)

    exchange_wait(cx, x, NX, cx_s, cx_r, at_x)
    cy[yh] = slot_sum(cx, NX)
    exchange_start(cy, yh, NYH, cy_s, cy_r, at_h)

    ag_recv(3)
    compute(3)

    exchange_wait(cy, yh, NYH, cy_s, cy_r, at_h)
    cg[z] = slot_sum(cy, NYH)
    exchange_start(cg, z, NZ, cg_s, cg_r, at_z)

    zphase(2)
    yphase(1)
    zphase(3)

    exchange_wait(cg, z, NZ, cg_s, cg_r, at_z)
    for k in range(CLASSES):
        for i in range(8):
            cross_ref[k : k + 1, 128 * i : 128 * (i + 1)] = cg[k, i : i + 1, :] / total

    yphase(2)
    yphase(3)
    for half in range(2):
        y_send(half).wait_recv()
        cov_ref[8 * half : 8 * half + 8, :] = (ykeep[half] + yr[half]) / (total - 1)

    ag_drain()
    for q in range(Q):
        for d in range(1, NX):
            x_copy(q, d).wait_send()
        for d in range(1, NZ):
            z_send(q, d).wait_send()
    for half in range(2):
        y_send(half).wait_send()


def body(activations, labels):
    tokens, width = activations.shape
    dma = pltpu.SemaphoreType.DMA
    vm = pltpu.VMEM
    tile = (8, 128)
    scratch = [
        vm((tokens, width), BF16),
        vm((tokens, width), BF16),
        vm((Q, NF, ROWS, tokens), BF16),
        vm((NF * ROWS, tokens), BF16),
        vm((Q, NX, NF * 8, width), F32),
        vm((Q, NX, NF * 8, width), BF16),
        vm((Q, NX - 1, NF * 8, width), BF16),
        vm((Q, NF, 8, width), F32),
        vm((Q, NZ, 16, width // 2), BF16),
        vm((Q, NZ - 1, 16, width // 2), BF16),
        vm((2, 8, width), F32),
        vm((2, 8, width), F32),
        vm((2, 8, width), F32),
        vm((NZ, *tile), F32),
        vm((NX, *tile), F32),
        vm((NYH, *tile), F32),
        vm((NF, *tile), F32),
        vm((1, width), F32),
        vm((NF, PANEL, PANEL), F32),
        vm((CLASSES, *tile), F32),
        vm((NZ, *tile), F32),
        vm((NX, *tile), F32),
        vm((NYH, *tile), F32),
        vm((NZ, *tile), F32),
        dma((2,)),
        dma((Q, NF)), dma((Q, NF)), dma((Q, NF)), dma((Q, NF)),
        dma((Q, NX - 1)), dma((Q, NX - 1)),
        dma((Q, NZ - 1)), dma((Q, NZ - 1)),
        dma((2,)), dma((2,)),
        dma((NZ,)), dma((NZ,)), dma((NX,)), dma((NX,)), dma((NYH,)), dma((NYH,)),
        dma((NF,)), dma((NF,)),
        dma((NZ,)), dma((NZ,)), dma((NX,)), dma((NX,)), dma((NYH,)), dma((NYH,)),
        dma((NZ,)), dma((NZ,)),
    ]
    out_rows = NF * PANEL // (NZ * NYH * NX)
    return pl.pallas_call(
        kernel,
        out_shape=(
            jax.ShapeDtypeStruct((out_rows, width), F32),
            jax.ShapeDtypeStruct((CLASSES, width), F32),
        ),
        in_specs=[
            pl.BlockSpec(memory_space=pl.ANY),
            pl.BlockSpec(memory_space=pltpu.VMEM),
        ],
        out_specs=(
            pl.BlockSpec(memory_space=pltpu.VMEM),
            pl.BlockSpec(memory_space=pltpu.VMEM),
        ),
        scratch_shapes=scratch,
        compiler_params=pltpu.CompilerParams(
            collective_id=0, has_side_effects=True, vmem_limit_bytes=48 * 2**20
        ),
        name="stats",
    )(activations, labels.reshape(1, tokens))


def solution(mesh):
    in_specs = (P("tok", "feat"), P("tok"))
    out_specs = (P("tok", "feat"), P(None, "feat"))
    return jax.shard_map(body, mesh=mesh, in_specs=in_specs, out_specs=out_specs, check_vma=False)
```

time: 763 us -> 101 us (0.13)
  the two profiles are of different devices: /device:TPU:8 before, /device:TPU:56 now
where the time goes in v1:
time: 101 us; the launch traced here: 100 us
  Pallas kernels  95.6 us (95%)
  local copies, waits for them, and re-layouts  4.12 us (4%)
    pallas_call x1, Pallas kernels, body(): pl.pallas_call(kernel, out_shape=(jax.ShapeDtypeStruct((out_rows, width),...  95.6 us
    unnamed x6, local copies, waits for them, and re-layouts  4.12 us

profile of v1, /device:TPU:56, one launch (start us, length us, event | category | flops | bytes accessed | tf_op | source)
XLA Modules:
  0.0 100.4 jit_solution(12114157214982695258)
XLA Ops:
  0.6 0.0 copy-start
  0.6 2.2 %copy-done = bf16[2048,1024]{1,0:T(8,128)(2,1)S(1)} copy-done((bf16[2048,1024]{1,0:T(8,128)(2,1)S(1)}, bf16[2048,1024]{1,0:T(8,128)(2,1)}, u32[]{:S(2)}) %copy-start) | copy-done | bytes 4194328
  2.8 0.0 copy-start.1
  2.8 0.7 copy-done.1
  3.5 95.6 %stats.1 = (f32[16,1024]{1,0:T(8,128)S(1)}, f32[8,1024]{1,0:T(8,128)S(1)}) custom-call(bf16[2048,1024]{1,0:T(8,128)(2,1)S(1)} %copy-done, s32[1,2048]{1,0:T(1,128)S(1)} %bitcast.1), custom_call_target="tpu_custom_call" | custom-call | tf_op jit(solution)/shard_map/stats/pallas_call | solution.py:417
  99.2 0.6 copy.6
  99.8 0.6 copy.7
Async XLA Ops:
  0.6 2.2 %copy-start = (bf16[2048,1024]{1,0:T(8,128)(2,1)S(1)}, bf16[2048,1024]{1,0:T(8,128)(2,1)}, u32[]{:S(2)}) copy-start(bf16[2048,1024]{1,0:T(8,128)(2,1)} %act_hbm.1) | copy-start | bytes 12582916
  2.8 0.7 copy-start.1

commit v2 on v1

--- a/solution.py
+++ b/solution.py
@@ -12,7 +12,7 @@
 NZ, NYH, NX = 8, 2, 4
 NY, NC = 4, 2
 NF = NY * NC
-Q = 4
+Q = 8
 ROWS = PANEL // Q
 MESH = pl.DeviceIdType.MESH
 F32 = jnp.float32
@@ -20,10 +20,19 @@
 
 
 def chunk_column(row):
-    q0 = (row >> 5) & 1
-    q1 = (row >> 6) & 1
-    x = (row >> 3) & 3
-    return 16 * (q0 * 4 + x) + 8 * q1 + (row & 7)
+    quarter = row >> 5
+    place = (row >> 2) & 7
+    return 16 * place + 4 * quarter + (row & 3)
+
+
+def fold(even, odd):
+    low = lax.broadcasted_iota(jnp.int32, even.shape, 0) < 4
+    return jnp.where(low, even, pltpu.roll(odd, 4, 0))
+
+
+def fold_upper(even, odd):
+    low = lax.broadcasted_iota(jnp.int32, even.shape, 0) < 4
+    return jnp.where(low, pltpu.roll(even, 4, 0), odd)
 
 
 def to_tile(row_value, ref):
@@ -32,8 +41,8 @@
 
 
 def kernel(
-    act_hbm, labels_ref, cov_ref, cross_ref,
-    abuf, cbuf, pan, lhs, accf, xs, xr, zsum, zs, zr, ykeep, ysend, yr,
+    act_hbm, labels_hbm, cov_ref, cross_ref,
+    abuf, labels_ref, cbuf, pan, lhs, accf, xs, xr, zsum, zs, zr, ykeep, ysend, yr,
     mz, mx, my, mf, mrow, mcol, crs, crr, cx, cy, cg,
     load_sem, ag_r, ag_right, ag_left, ag_part,
     x_s, x_r, z_s, z_r, y_s, y_r,
@@ -68,8 +77,10 @@
     rest = pltpu.make_async_copy(
         act_hbm.at[:, pl.ds(PANEL, width - PANEL)],
         abuf.at[:, pl.ds(PANEL, width - PANEL)], load_sem.at[1])
+    tags = pltpu.make_async_copy(labels_hbm, labels_ref, load_sem.at[2])
     first.start()
     rest.start()
+    tags.start()
 
     barrier = pltpu.get_barrier_semaphore()
     for d in range(1, NF):
@@ -93,15 +104,6 @@
         for q in range(Q):
             pan[q, feat, :, i * part : (i + 1) * part] = turned[q * ROWS : (q + 1) * ROWS, :]
 
-    rest.wait()
-
-    def add_rows(i, carry):
-        block = abuf[pl.ds(pl.multiple_of(i * 64, 64), 64), :].astype(F32)
-        return carry + jnp.sum(block.reshape(8, 8, width), axis=0)
-
-    sums = lax.fori_loop(0, tokens // 64, add_rows, jnp.zeros((8, width), F32))
-    to_tile(jnp.sum(sums, axis=0, keepdims=True), mz.at[z])
-
     pl.semaphore_wait(barrier, (NF - 1) + (NZ - 1) + (NX - 1) + 1)
 
     def panel_copy(q, f, device, send):
@@ -127,30 +129,34 @@
 
         go_part(q, feat).start()
 
-    def ag_recv(q):
-        for k in range(1, NY):
-            @pl.when(y >= k)
+    def ag_recv_step(q, k):
+        @pl.when(y >= k)
+        def _():
+            f = feat - NC * k
+            go_part(q, f).wait_recv()
+
+            @pl.when(y < NY - 1)
             def _():
-                f = feat - NC * k
-                go_part(q, f).wait_recv()
-
-                @pl.when(y < NY - 1)
-                def _():
-                    go_right(q, f).start()
-
-                go_part(q, f).start()
-
-            @pl.when(y + k < NY)
+                go_right(q, f).start()
+
+            go_part(q, f).start()
+
+        @pl.when(y + k < NY)
+        def _():
+            f = feat + NC * k
+            go_part(q, f).wait_recv()
+
+            @pl.when(y > 0)
             def _():
-                f = feat + NC * k
-                go_part(q, f).wait_recv()
-
-                @pl.when(y > 0)
-                def _():
-                    go_left(q, f).start()
-
-                go_part(q, f).start()
-
+                go_left(q, f).start()
+
+            go_part(q, f).start()
+
+    def ag_recv(q, first_step=1):
+        for k in range(first_step, NY):
+            ag_recv_step(q, k)
+
+    def ag_recv_part(q):
         for yy in range(NY):
             go_part(q, yy * NC + 1 - c).wait_recv()
 
@@ -202,7 +208,12 @@
             value = value + buf[i]
         return value
 
+    half = width // 2
+    quarter = width // 4
+    side_a, side_b = pl.ds(0, half), pl.ds(half, half)
+
     def compute(q):
+        ag_recv_part(q)
         for f in range(NF):
             block = pan[q, f].astype(F32) - mcol[f, q * ROWS : (q + 1) * ROWS, 0:1]
             lhs[f * ROWS : (f + 1) * ROWS, :] = block.astype(BF16)
@@ -210,71 +221,96 @@
         def columns(n, carry):
             at = pl.ds(pl.multiple_of(n * 256, 256), 256)
             acc = jnp.dot(lhs[...], cbuf[:, at], preferred_element_type=F32)
-            acc = acc.reshape(NF, NX, 8, 256)
+            acc = acc.reshape(NF // 2, 2, NX // 2, 8, 256)
             for xx in range(NX):
-                slab = acc[:, xx].reshape(NF * 8, 256)
+                join = fold_upper if xx % 2 else fold
+                rows = [join(acc[i, 0, xx // 2], acc[i, 1, xx // 2]) for i in range(NF // 2)]
+                slab = jnp.concatenate(rows, axis=0)
                 accf[q, xx, :, at] = slab
                 xs[q, xx, :, at] = slab.astype(BF16)
             return carry
 
         lax.fori_loop(0, width // 256, columns, 0)
-        for d in range(1, NX):
-            x_copy(q, d).start()
-
-    def x_copy(q, d):
-        to = (x + d) % NX
-        return remote(xs.at[q, to], xr.at[q, d - 1], x_s.at[q, d - 1], x_r.at[q, d - 1], dev(xx=to))
+        for m in range(4):
+            x_copy(q, m).start()
+
+    right, left, across = (x + 1) % NX, (x + NX - 1) % NX, (x + 2) % NX
+
+    def x_copy(q, m):
+        slab = (across, across, right, left, right, left)[m]
+        side = (side_a, side_b, side_b, side_a, side_a, side_b)[m]
+        to = (right, left)[m % 2]
+        return remote(xs.at[q, slab, :, side], xr.at[q, m], x_s.at[q, m], x_r.at[q, m], dev(xx=to))
+
+    def xphase(q):
+        for m, slab, side in ((4, right, side_a), (5, left, side_b)):
+            x_copy(q, m - 4).wait_recv()
+            xs[q, slab, :, side] = (accf[q, slab, :, side] + xr[q, m - 4].astype(F32)).astype(BF16)
+            x_copy(q, m).start()
 
     def z_send(q, d):
         to = (z + d) % NZ
         return remote(zs.at[q, to], zr.at[q, d - 1], z_s.at[q, d - 1], z_r.at[q, d - 1], dev(zz=to))
 
     def zphase(q):
-        for d in range(1, NX):
-            x_copy(q, d).wait_recv()
+        for m in range(2, 6):
+            x_copy(q, m).wait_recv()
+        value_a = accf[q, x, :, side_a] + xr[q, 4].astype(F32) + xr[q, 3].astype(F32)
+        value_b = accf[q, x, :, side_b] + xr[q, 2].astype(F32) + xr[q, 5].astype(F32)
         for f in range(NF):
-            at = slice(f * 8, f * 8 + 8)
-            value = accf[q, x, at, :]
-            for d in range(NX - 1):
-                value = value + xr[q, d, at, :].astype(F32)
-            zsum[q, f] = value
-            half = width // 2
-            zs[q, f] = jnp.concatenate([value[:, :half], value[:, half:]], axis=0).astype(BF16)
+            join = fold_upper if f % 2 else fold
+            at = slice(f // 2 * 8, f // 2 * 8 + 8)
+            packed = jnp.concatenate(
+                [join(v[at, :quarter], v[at, quarter:]) for v in (value_a, value_b)], axis=0)
+            zsum[q, f] = packed
+            zs[q, f] = packed.astype(BF16)
         for d in range(1, NZ):
             z_send(q, d).start()
 
-    def y_send(half):
-        return remote(ysend.at[half], yr.at[half], y_s.at[half], y_r.at[half], dev(hh=1 - yh))
+    def y_send(n):
+        return remote(ysend.at[n], yr.at[n], y_s.at[n], y_r.at[n], dev(hh=1 - yh))
 
     def yphase(q):
         for d in range(1, NZ):
             z_send(q, d).wait_recv()
-        parts = jnp.zeros((16, width // 2), F32)
+        value = zsum[q, z]
         for d in range(NZ - 1):
-            parts = parts + zr[q, d].astype(F32)
-        value = zsum[q, z] + jnp.concatenate([parts[:8], parts[8:]], axis=1)
-        half = q // 2
+            value = value + zr[q, d].astype(F32)
+        n = q // 2
 
         @pl.when(yh == q % 2)
         def _():
-            ykeep[half] = value
+            ykeep[n] = value
 
         @pl.when(yh != q % 2)
         def _():
-            ysend[half] = value
-            y_send(half).start()
+            ysend[n] = value
+            y_send(n).start()
+
+    for q in range(4):
+        ag_own(q)
+    rest.wait()
+
+    def add_rows(i, carry):
+        block = abuf[pl.ds(pl.multiple_of(i * 64, 64), 64), :].astype(F32)
+        return carry + jnp.sum(block.reshape(8, 8, width), axis=0)
+
+    sums = lax.fori_loop(0, tokens // 64, add_rows, jnp.zeros((8, width), F32))
+    to_tile(jnp.sum(sums, axis=0, keepdims=True), mz.at[z])
+
 
     exchange_start(mz, z, NZ, mz_s, mz_r, at_z)
-    ag_own(0)
-    ag_own(1)
+    ag_recv_step(0, 1)
     exchange_wait(mz, z, NZ, mz_s, mz_r, at_z)
     mx[x] = slot_sum(mz, NZ)
     exchange_start(mx, x, NX, mx_s, mx_r, at_x)
-    ag_recv(0)
+    ag_recv(0, 2)
+    ag_own(4)
     exchange_wait(mx, x, NX, mx_s, mx_r, at_x)
     my[yh] = slot_sum(mx, NX)
     exchange_start(my, yh, NYH, my_s, my_r, at_h)
-    ag_own(2)
+    ag_recv(1)
+    ag_own(5)
     exchange_wait(my, yh, NYH, my_s, my_r, at_h)
     mean = slot_sum(my, NYH) / total
     mf[feat] = mean
@@ -288,17 +324,22 @@
         return carry
 
     lax.fori_loop(0, tokens // 64, center, 0)
-    ag_recv(1)
-    ag_own(3)
+    ag_recv(2)
+    ag_own(6)
 
     exchange_wait(mf, feat, NF, mf_s, mf_r, at_f)
     for f in range(NF):
         value = jnp.where(pick, mf[f, 0:1, :], 0.0)
         mcol[f] = jnp.broadcast_to(jnp.sum(value, axis=1, keepdims=True), (PANEL, PANEL))
 
+    ag_recv(3)
+    ag_own(7)
     compute(0)
     compute(1)
-
+    ag_recv(4)
+    compute(2)
+
+    tags.wait()
     classes = lax.broadcasted_iota(jnp.int32, (16, tokens), 0)
     onehot = jnp.where(classes == labels_ref[...], 1.0, 0.0).astype(BF16)
 
@@ -324,9 +365,13 @@
     for d in range(1, NZ):
         class_copy(d).start()
 
+    xphase(0)
+    xphase(1)
+    compute(3)
+    ag_recv(5)
     zphase(0)
-    ag_recv(2)
-    compute(2)
+    xphase(2)
+    compute(4)
 
     for d in range(1, NZ):
         class_copy(d).wait_send()
@@ -335,42 +380,59 @@
     exchange_start(cx, x, NX, cx_s, cx_r, at_x)
 
     zphase(1)
-    yphase(0)
+    xphase(3)
+    ag_recv(6)
+    compute(5)
+    zphase(2)
+    xphase(4)
 
     exchange_wait(cx, x, NX, cx_s, cx_r, at_x)
     cy[yh] = slot_sum(cx, NX)
     exchange_start(cy, yh, NYH, cy_s, cy_r, at_h)
 
-    ag_recv(3)
-    compute(3)
-
+    ag_recv(7)
+    compute(6)
+    zphase(3)
+    xphase(5)
+    compute(7)
+
+    zphase(4)
+    xphase(6)
     exchange_wait(cy, yh, NYH, cy_s, cy_r, at_h)
     cg[z] = slot_sum(cy, NYH)
     exchange_start(cg, z, NZ, cg_s, cg_r, at_z)
-
-    zphase(2)
+    zphase(5)
+    xphase(7)
+    zphase(6)
+    yphase(0)
     yphase(1)
-    zphase(3)
+    yphase(2)
+    zphase(7)
+    yphase(3)
+    yphase(4)
+    yphase(5)
+    yphase(6)
 
     exchange_wait(cg, z, NZ, cg_s, cg_r, at_z)
     for k in range(CLASSES):
         for i in range(8):
             cross_ref[k : k + 1, 128 * i : 128 * (i + 1)] = cg[k, i : i + 1, :] / total
 
-    yphase(2)
-    yphase(3)
-    for half in range(2):
-        y_send(half).wait_recv()
-        cov_ref[8 * half : 8 * half + 8, :] = (ykeep[half] + yr[half]) / (total - 1)
+    yphase(7)
+    for n in range(Q // 2):
+        y_send(n).wait_recv()
+        value = (ykeep[n] + yr[n]) / (total - 1)
+        for i in range(4):
+            cov_ref[4 * n : 4 * n + 4, quarter * i : quarter * (i + 1)] = value[4 * i : 4 * i + 4, :]
 
     ag_drain()
     for q in range(Q):
-        for d in range(1, NX):
-            x_copy(q, d).wait_send()
+        for m in range(6):
+            x_copy(q, m).wait_send()
         for d in range(1, NZ):
             z_send(q, d).wait_send()
-    for half in range(2):
-        y_send(half).wait_send()
+    for n in range(Q // 2):
+        y_send(n).wait_send()
 
 
 def body(activations, labels):
@@ -380,18 +442,19 @@
     tile = (8, 128)
     scratch = [
         vm((tokens, width), BF16),
+        vm((1, tokens), jnp.int32),
         vm((tokens, width), BF16),
         vm((Q, NF, ROWS, tokens), BF16),
         vm((NF * ROWS, tokens), BF16),
-        vm((Q, NX, NF * 8, width), F32),
-        vm((Q, NX, NF * 8, width), BF16),
-        vm((Q, NX - 1, NF * 8, width), BF16),
-        vm((Q, NF, 8, width), F32),
-        vm((Q, NZ, 16, width // 2), BF16),
-        vm((Q, NZ - 1, 16, width // 2), BF16),
-        vm((2, 8, width), F32),
-        vm((2, 8, width), F32),
-        vm((2, 8, width), F32),
+        vm((Q, NX, NF * 4, width), F32),
+        vm((Q, NX, NF * 4, width), BF16),
+        vm((Q, 6, NF * 4, width // 2), BF16),
+        vm((Q, NF, 16, width // 4), F32),
+        vm((Q, NZ, 16, width // 4), BF16),
+        vm((Q, NZ - 1, 16, width // 4), BF16),
+        vm((Q // 2, 16, width // 4), F32),
+        vm((Q // 2, 16, width // 4), F32),
+        vm((Q // 2, 16, width // 4), F32),
         vm((NZ, *tile), F32),
         vm((NX, *tile), F32),
         vm((NYH, *tile), F32),
@@ -403,11 +466,11 @@
         vm((NX, *tile), F32),
         vm((NYH, *tile), F32),
         vm((NZ, *tile), F32),
-        dma((2,)),
+        dma((3,)),
         dma((Q, NF)), dma((Q, NF)), dma((Q, NF)), dma((Q, NF)),
-        dma((Q, NX - 1)), dma((Q, NX - 1)),
+        dma((Q, 6)), dma((Q, 6)),
         dma((Q, NZ - 1)), dma((Q, NZ - 1)),
-        dma((2,)), dma((2,)),
+        dma((Q // 2,)), dma((Q // 2,)),
         dma((NZ,)), dma((NZ,)), dma((NX,)), dma((NX,)), dma((NYH,)), dma((NYH,)),
         dma((NF,)), dma((NF,)),
         dma((NZ,)), dma((NZ,)), dma((NX,)), dma((NX,)), dma((NYH,)), dma((NYH,)),
@@ -422,7 +485,7 @@
         ),
         in_specs=[
             pl.BlockSpec(memory_space=pl.ANY),
-            pl.BlockSpec(memory_space=pltpu.VMEM),
+            pl.BlockSpec(memory_space=pl.ANY),
         ],
         out_specs=(
             pl.BlockSpec(memory_space=pltpu.VMEM),
@@ -430,7 +493,7 @@
         ),
         scratch_shapes=scratch,
         compiler_params=pltpu.CompilerParams(
-            collective_id=0, has_side_effects=True, vmem_limit_bytes=48 * 2**20
+            collective_id=0, has_side_effects=True, vmem_limit_bytes=60 * 2**20
         ),
         name="stats",
     )(activations, labels.reshape(1, tokens))

time: 101 us -> 92.8 us (0.919)
  Pallas kernels: 95.6 us -> 89.1 us
  local copies, waits for them, and re-layouts: 4.12 us -> 2.85 us
    pallas_call x1, Pallas kernels: 95.6 us -> 89.1 us  [body(): pl.pallas_call(kernel, out_shape=(jax.ShapeDtypeStruct((out_rows, width),...]
    unnamed x6 -> x2, local copies, waits for them, and re-layouts: 4.12 us -> 2.85 us
where the time goes in v2:
time: 92.8 us; the launch traced here: 92.6 us
  Pallas kernels  89.1 us (96%)
  local copies, waits for them, and re-layouts  2.85 us (3%)
    pallas_call x1, Pallas kernels, body(): pl.pallas_call(kernel, out_shape=(jax.ShapeDtypeStruct((out_rows, width),...  89.1 us
    unnamed x2, local copies, waits for them, and re-layouts  2.85 us

profile of v2, /device:TPU:56, one launch (start us, length us, event | category | flops | bytes accessed | tf_op | source)
XLA Modules:
  0.0 92.6 jit_solution(11711944415107659276)
XLA Ops:
  0.6 89.1 %stats.1 = (f32[16,1024]{1,0:T(8,128)}, f32[8,1024]{1,0:T(8,128)}) custom-call(bf16[2048,1024]{1,0:T(8,128)(2,1)} %act_hbm.1, s32[1,2048]{1,0:T(1,128)} %bitcast.1), custom_call_target="tpu_custom_call" | custom-call | tf_op jit(solution)/shard_map/stats/pallas_call | solution.py:480
  89.7 1.5 %copy.6 = f32[16,1024]{1,0:T(8,128)} copy(f32[16,1024]{1,0:T(8,128)} %get-tuple-element.4) | data formatting | bytes 131072
  91.2 1.4 %copy.7 = f32[8,1024]{1,0:T(8,128)} copy(f32[8,1024]{1,0:T(8,128)} %get-tuple-element.5) | data formatting | bytes 65536

commit v3 on v2

--- a/solution.py
+++ b/solution.py
@@ -44,8 +44,7 @@
     act_hbm, labels_hbm, cov_ref, cross_ref,
     abuf, labels_ref, cbuf, pan, lhs, accf, xs, xr, zsum, zs, zr, ykeep, ysend, yr,
     mz, mx, my, mf, mrow, mcol, crs, crr, cx, cy, cg,
-    load_sem, ag_r, ag_right, ag_left, ag_part,
-    x_s, x_r, z_s, z_r, y_s, y_r,
+    load_sem, ag_r, ag_pr, ag_s, x_s, x_r, z_s, z_r, y_s, y_r,
     mz_s, mz_r, mx_s, mx_r, my_s, my_r, mf_s, mf_r,
     cr_s, cr_r, cx_s, cx_r, cy_s, cy_r, cg_s, cg_r,
 ):
@@ -102,93 +101,81 @@
             select, abuf[i * part : (i + 1) * part, :PANEL],
             (((1,), (1,)), ((), ())), preferred_element_type=F32).astype(BF16)
         for q in range(Q):
-            pan[q, feat, :, i * part : (i + 1) * part] = turned[q * ROWS : (q + 1) * ROWS, :]
+            pan[q, c, y, :, i * part : (i + 1) * part] = turned[q * ROWS : (q + 1) * ROWS, :]
 
     pl.semaphore_wait(barrier, (NF - 1) + (NZ - 1) + (NX - 1) + 1)
 
-    def panel_copy(q, f, device, send):
-        return remote(pan.at[q, f], pan.at[q, f], send.at[q, f], ag_r.at[q, f], device)
-
-    def go_right(q, f):
-        return panel_copy(q, f, dev(ff=(feat + NC) % NF), ag_right)
-
-    def go_left(q, f):
-        return panel_copy(q, f, dev(ff=(feat + NF - NC) % NF), ag_left)
-
-    def go_part(q, f):
-        return panel_copy(q, f, dev(ff=y * NC + 1 - c), ag_part)
+    def panel_copy(q, yy, to, n):
+        to = jnp.clip(to, 0, NY - 1)
+        return remote(
+            pan.at[q, c, yy], pan.at[q, c, yy], ag_s.at[n], ag_r.at[q, yy], dev(ff=to * NC + c))
+
+    def share_copy(q, yy):
+        return remote(pan.at[q, c, yy], pan.at[q, c, yy], ag_s.at[5], ag_pr.at[q], dev(ff=y * NC + 1 - c))
 
     def ag_own(q):
-        @pl.when(y < NY - 1)
+        for n, step in enumerate((1, -1, 2, -2)):
+            @pl.when((y + step >= 0) & (y + step < NY))
+            def _():
+                panel_copy(q, y, y + step, n).start()
+
+        share_copy(q, y).start()
+
+    def got(q, yy):
+        panel_copy(q, yy, y, 0).wait_recv()
+        share_copy(q, yy).start()
+
+    def forward(q):
+        @pl.when(y == 2)
         def _():
-            go_right(q, feat).start()
-
-        @pl.when(y > 0)
+            got(q, 0)
+            panel_copy(q, 0, 3, 4).start()
+
+        @pl.when(y == 1)
         def _():
-            go_left(q, feat).start()
-
-        go_part(q, feat).start()
-
-    def ag_recv_step(q, k):
-        @pl.when(y >= k)
+            got(q, 3)
+            panel_copy(q, 3, 0, 4).start()
+
+    def share(q):
+        for step in (1, -1, 2, -2, 3, -3):
+            inside = (y + step >= 0) & (y + step < NY)
+            if abs(step) == 2:
+                inside = inside & ((y == 0) | (y == NY - 1))
+
+            @pl.when(inside)
+            def _():
+                got(q, y + step)
+
+    def ag_recv_part(q):
+        remote(pan.at[q, 1 - c], pan.at[q, 1 - c], ag_s.at[5], ag_pr.at[q], dev(ff=y * NC + 1 - c)).wait_recv()
+
+    def ag_drain():
+        own = pan.at[:, c, y]
+        for n, step in enumerate((1, -1, 2, -2)):
+            @pl.when((y + step >= 0) & (y + step < NY))
+            def _():
+                remote(own, own, ag_s.at[n], ag_r.at[0, 0], dev(ff=y * NC + 1 - c)).wait_send()
+
+        @pl.when((y == 1) | (y == 2))
         def _():
-            f = feat - NC * k
-            go_part(q, f).wait_recv()
-
-            @pl.when(y < NY - 1)
-            def _():
-                go_right(q, f).start()
-
-            go_part(q, f).start()
-
-        @pl.when(y + k < NY)
-        def _():
-            f = feat + NC * k
-            go_part(q, f).wait_recv()
-
-            @pl.when(y > 0)
-            def _():
-                go_left(q, f).start()
-
-            go_part(q, f).start()
-
-    def ag_recv(q, first_step=1):
-        for k in range(first_step, NY):
-            ag_recv_step(q, k)
-
-    def ag_recv_part(q):
-        for yy in range(NY):
-            go_part(q, yy * NC + 1 - c).wait_recv()
-
-    def ag_drain():
-        for q in range(Q):
-            for yy in range(NY):
-                f = yy * NC + c
-
-                @pl.when((y < NY - 1) & (y >= yy))
-                def _():
-                    go_right(q, f).wait_send()
-
-                @pl.when((y > 0) & (y <= yy))
-                def _():
-                    go_left(q, f).wait_send()
-
-                go_part(q, f).wait_send()
-
-    def z_copy(buf, src, dst, send, recv, d):
-        to = (z + d) % NZ
-        return remote(src, dst, send.at[to], recv.at[z], dev(zz=to))
+            remote(own, own, ag_s.at[4], ag_r.at[0, 0], dev(ff=y * NC + 1 - c)).wait_send()
+
+        shared = pan.at[:, c]
+        remote(shared, shared, ag_s.at[5], ag_r.at[0, 0], dev(ff=y * NC + 1 - c)).wait_send()
+
+    def far_first(n):
+        return sorted(range(1, n), key=lambda d: -min(d, n - d))
 
     def exchange_start(buf, own, n, send, recv, where):
-        for d in range(1, n):
+        for d in far_first(n):
             to = (own + d) % n
-            remote(buf.at[own], buf.at[own], send.at[to], recv.at[own], where(to)).start()
+            remote(buf.at[own], buf.at[own], send, recv, where(to)).start()
 
     def exchange_wait(buf, own, n, send, recv, where):
-        for d in range(1, n):
-            to = (own + d) % n
-            remote(buf.at[own], buf.at[own], send.at[to], recv.at[own], where(to)).wait_send()
-            remote(buf.at[to], buf.at[to], send.at[to], recv.at[to], where(to)).wait_recv()
+        rest_of = buf.at[pl.ds(0, n - 1)]
+        every = remote(rest_of, rest_of, send, recv, where((own + 1) % n))
+        every.wait_send()
+        every.wait_recv()
 
     def at_z(to):
         return dev(zz=to)
@@ -215,7 +202,7 @@
     def compute(q):
         ag_recv_part(q)
         for f in range(NF):
-            block = pan[q, f].astype(F32) - mcol[f, q * ROWS : (q + 1) * ROWS, 0:1]
+            block = pan[q, f % NC, f // NC].astype(F32) - mcol[f, q * ROWS : (q + 1) * ROWS, 0:1]
             lhs[f * ROWS : (f + 1) * ROWS, :] = block.astype(BF16)
 
         def columns(n, carry):
@@ -240,7 +227,7 @@
         slab = (across, across, right, left, right, left)[m]
         side = (side_a, side_b, side_b, side_a, side_a, side_b)[m]
         to = (right, left)[m % 2]
-        return remote(xs.at[q, slab, :, side], xr.at[q, m], x_s.at[q, m], x_r.at[q, m], dev(xx=to))
+        return remote(xs.at[q, slab, :, side], xr.at[q, m], x_s.at[m], x_r.at[q, min(m, 2)], dev(xx=to))
 
     def xphase(q):
         for m, slab, side in ((4, right, side_a), (5, left, side_b)):
@@ -250,11 +237,11 @@
 
     def z_send(q, d):
         to = (z + d) % NZ
-        return remote(zs.at[q, to], zr.at[q, d - 1], z_s.at[q, d - 1], z_r.at[q, d - 1], dev(zz=to))
+        return remote(zs.at[q, to], zr.at[q, d - 1], z_s, z_r.at[q], dev(zz=to))
 
     def zphase(q):
-        for m in range(2, 6):
-            x_copy(q, m).wait_recv()
+        last = xr.at[q, 2:6]
+        remote(last, last, x_s.at[2], x_r.at[q, 2], dev(xx=right)).wait_recv()
         value_a = accf[q, x, :, side_a] + xr[q, 4].astype(F32) + xr[q, 3].astype(F32)
         value_b = accf[q, x, :, side_b] + xr[q, 2].astype(F32) + xr[q, 5].astype(F32)
         for f in range(NF):
@@ -264,15 +251,14 @@
                 [join(v[at, :quarter], v[at, quarter:]) for v in (value_a, value_b)], axis=0)
             zsum[q, f] = packed
             zs[q, f] = packed.astype(BF16)
-        for d in range(1, NZ):
+        for d in far_first(NZ):
             z_send(q, d).start()
 
     def y_send(n):
-        return remote(ysend.at[n], yr.at[n], y_s.at[n], y_r.at[n], dev(hh=1 - yh))
+        return remote(ysend.at[n], yr.at[n], y_s, y_r, dev(hh=1 - yh))
 
     def yphase(q):
-        for d in range(1, NZ):
-            z_send(q, d).wait_recv()
+        remote(zr.at[q], zr.at[q], z_s, z_r.at[q], dev(zz=(z + 1) % NZ)).wait_recv()
         value = zsum[q, z]
         for d in range(NZ - 1):
             value = value + zr[q, d].astype(F32)
@@ -300,17 +286,15 @@
 
 
     exchange_start(mz, z, NZ, mz_s, mz_r, at_z)
-    ag_recv_step(0, 1)
     exchange_wait(mz, z, NZ, mz_s, mz_r, at_z)
     mx[x] = slot_sum(mz, NZ)
     exchange_start(mx, x, NX, mx_s, mx_r, at_x)
-    ag_recv(0, 2)
-    ag_own(4)
+    forward(0)
     exchange_wait(mx, x, NX, mx_s, mx_r, at_x)
     my[yh] = slot_sum(mx, NX)
     exchange_start(my, yh, NYH, my_s, my_r, at_h)
-    ag_recv(1)
-    ag_own(5)
+    ag_own(4)
+    forward(1)
     exchange_wait(my, yh, NYH, my_s, my_r, at_h)
     mean = slot_sum(my, NYH) / total
     mf[feat] = mean
@@ -324,20 +308,24 @@
         return carry
 
     lax.fori_loop(0, tokens // 64, center, 0)
-    ag_recv(2)
-    ag_own(6)
+    ag_own(5)
+    forward(2)
+    forward(3)
 
     exchange_wait(mf, feat, NF, mf_s, mf_r, at_f)
     for f in range(NF):
         value = jnp.where(pick, mf[f, 0:1, :], 0.0)
         mcol[f] = jnp.broadcast_to(jnp.sum(value, axis=1, keepdims=True), (PANEL, PANEL))
 
-    ag_recv(3)
+    ag_own(6)
+    forward(4)
+    share(0)
+    share(1)
     ag_own(7)
     compute(0)
+    forward(5)
+    share(2)
     compute(1)
-    ag_recv(4)
-    compute(2)
 
     tags.wait()
     classes = lax.broadcasted_iota(jnp.int32, (16, tokens), 0)
@@ -353,86 +341,72 @@
 
     lax.fori_loop(0, width // 256, class_columns, 0)
     crr[z] = crs[z]
-
-    def class_copy(d):
+    for d in far_first(NZ):
         to = (z + d) % NZ
-        return remote(crs.at[to], crr.at[z], cr_s.at[to], cr_r.at[z], at_z(to))
-
-    def class_from(d):
-        to = (z + d) % NZ
-        return remote(crs.at[to], crr.at[to], cr_s.at[to], cr_r.at[to], at_z(to))
-
-    for d in range(1, NZ):
-        class_copy(d).start()
-
+        remote(crs.at[to], crr.at[z], cr_s, cr_r, at_z(to)).start()
+
+    forward(6)
+    share(3)
+    compute(2)
     xphase(0)
+    share(4)
+    compute(3)
     xphase(1)
-    compute(3)
-    ag_recv(5)
+    forward(7)
     zphase(0)
-    xphase(2)
-    compute(4)
-
-    for d in range(1, NZ):
-        class_copy(d).wait_send()
-        class_from(d).wait_recv()
+    exchange_wait(crr, z, NZ, cr_s, cr_r, at_z)
     cx[x] = slot_sum(crr, NZ)
     exchange_start(cx, x, NX, cx_s, cx_r, at_x)
-
+    share(5)
+    compute(4)
+    xphase(2)
     zphase(1)
-    xphase(3)
-    ag_recv(6)
-    compute(5)
-    zphase(2)
-    xphase(4)
-
     exchange_wait(cx, x, NX, cx_s, cx_r, at_x)
     cy[yh] = slot_sum(cx, NX)
     exchange_start(cy, yh, NYH, cy_s, cy_r, at_h)
-
-    ag_recv(7)
+    share(6)
+    compute(5)
+    xphase(3)
+    zphase(2)
+    exchange_wait(cy, yh, NYH, cy_s, cy_r, at_h)
+    cg[z] = slot_sum(cy, NYH)
+    exchange_start(cg, z, NZ, cg_s, cg_r, at_z)
+    share(7)
     compute(6)
+    xphase(4)
     zphase(3)
     xphase(5)
     compute(7)
-
     zphase(4)
     xphase(6)
-    exchange_wait(cy, yh, NYH, cy_s, cy_r, at_h)
-    cg[z] = slot_sum(cy, NYH)
-    exchange_start(cg, z, NZ, cg_s, cg_r, at_z)
     zphase(5)
     xphase(7)
     zphase(6)
     yphase(0)
     yphase(1)
     yphase(2)
-    zphase(7)
     yphase(3)
     yphase(4)
-    yphase(5)
-    yphase(6)
-
     exchange_wait(cg, z, NZ, cg_s, cg_r, at_z)
     for k in range(CLASSES):
         for i in range(8):
             cross_ref[k : k + 1, 128 * i : 128 * (i + 1)] = cg[k, i : i + 1, :] / total
-
+    zphase(7)
+    yphase(5)
+    yphase(6)
     yphase(7)
+
+    ag_drain()
+    for m in range(6):
+        sent = xr.at[:, m]
+        remote(sent, sent, x_s.at[m], x_r.at[0, 0], dev(xx=right)).wait_send()
+    remote(zr, zr, z_s, z_r.at[0], dev(zz=(z + 1) % NZ)).wait_send()
+    remote(ysend, ysend, y_s, y_r, dev(hh=1 - yh)).wait_send()
+    remote(yr, yr, y_s, y_r, dev(hh=1 - yh)).wait_recv()
     for n in range(Q // 2):
-        y_send(n).wait_recv()
         value = (ykeep[n] + yr[n]) / (total - 1)
         for i in range(4):
             cov_ref[4 * n : 4 * n + 4, quarter * i : quarter * (i + 1)] = value[4 * i : 4 * i + 4, :]
-
-    ag_drain()
-    for q in range(Q):
-        for m in range(6):
-            x_copy(q, m).wait_send()
-        for d in range(1, NZ):
-            z_send(q, d).wait_send()
-    for n in range(Q // 2):
-        y_send(n).wait_send()
 
 
 def body(activations, labels):
@@ -444,7 +418,7 @@
         vm((tokens, width), BF16),
         vm((1, tokens), jnp.int32),
         vm((tokens, width), BF16),
-        vm((Q, NF, ROWS, tokens), BF16),
+        vm((Q, NC, NY, ROWS, tokens), BF16),
         vm((NF * ROWS, tokens), BF16),
         vm((Q, NX, NF * 4, width), F32),
         vm((Q, NX, NF * 4, width), BF16),
@@ -467,15 +441,11 @@
         vm((NYH, *tile), F32),
         vm((NZ, *tile), F32),
         dma((3,)),
-        dma((Q, NF)), dma((Q, NF)), dma((Q, NF)), dma((Q, NF)),
-        dma((Q, 6)), dma((Q, 6)),
-        dma((Q, NZ - 1)), dma((Q, NZ - 1)),
-        dma((Q // 2,)), dma((Q // 2,)),
-        dma((NZ,)), dma((NZ,)), dma((NX,)), dma((NX,)), dma((NYH,)), dma((NYH,)),
-        dma((NF,)), dma((NF,)),
-        dma((NZ,)), dma((NZ,)), dma((NX,)), dma((NX,)), dma((NYH,)), dma((NYH,)),
-        dma((NZ,)), dma((NZ,)),
-    ]
+        dma((Q, NY)), dma((Q,)), dma((6,)),
+        dma((6,)), dma((Q, 3)),
+        dma(()), dma((Q,)),
+        dma(()), dma(()),
+    ] + [dma(())] * 16
     out_rows = NF * PANEL // (NZ * NYH * NX)
     return pl.pallas_call(
         kernel,

time: 92.8 us -> 84.3 us (0.908)
  Pallas kernels: 89.1 us -> 80.5 us
    pallas_call x1, Pallas kernels: 89.1 us -> 80.5 us  [body(): pl.pallas_call(kernel, out_shape=(jax.ShapeDtypeStruct((out_rows, width),...]
where the time goes in v3:
time: 84.3 us; the launch traced here: 84 us
  Pallas kernels  80.5 us (95%)
  local copies, waits for them, and re-layouts  2.85 us (3%)
    pallas_call x1, Pallas kernels, body(): pl.pallas_call(kernel, out_shape=(jax.ShapeDtypeStruct((out_rows, width),...  80.5 us
    unnamed x2, local copies, waits for them, and re-layouts  2.85 us

profile of v3, /device:TPU:56, one launch (start us, length us, event | category | flops | bytes accessed | tf_op | source)
XLA Modules:
  0.0 84.0 jit_solution(12319095501812279314)
XLA Ops:
  0.6 80.5 %stats.1 = (f32[16,1024]{1,0:T(8,128)}, f32[8,1024]{1,0:T(8,128)}) custom-call(bf16[2048,1024]{1,0:T(8,128)(2,1)} %act_hbm.1, s32[1,2048]{1,0:T(1,128)} %bitcast.1), custom_call_target="tpu_custom_call" | custom-call | tf_op jit(solution)/shard_map/stats/pallas_call | solution.py:450
  81.2 1.5 %copy.6 = f32[16,1024]{1,0:T(8,128)} copy(f32[16,1024]{1,0:T(8,128)} %get-tuple-element.4) | data formatting | bytes 131072
  82.7 1.4 %copy.7 = f32[8,1024]{1,0:T(8,128)} copy(f32[8,1024]{1,0:T(8,128)} %get-tuple-element.5) | data formatting | bytes 65536

commit v4 on v3

--- a/solution.py
+++ b/solution.py
@@ -71,6 +71,12 @@
             device_id=device, device_id_type=MESH,
         )
 
+    barrier = pltpu.get_barrier_semaphore()
+    greet = [dev(zz=(z + d) % NZ) for d in (4, 3, 5, 2, 6, 1, 7)] + [dev(hh=1 - yh)]
+    greet += [dev(ff=(feat + d) % NF) for d in range(1, NF)] + [dev(xx=(x + d) % NX) for d in range(1, NX)]
+    for device in greet:
+        pl.semaphore_signal(barrier, inc=1, device_id=device, device_id_type=MESH)
+
     first = pltpu.make_async_copy(
         act_hbm.at[:, pl.ds(0, PANEL)], abuf.at[:, pl.ds(0, PANEL)], load_sem.at[0])
     rest = pltpu.make_async_copy(
@@ -80,15 +86,6 @@
     first.start()
     rest.start()
     tags.start()
-
-    barrier = pltpu.get_barrier_semaphore()
-    for d in range(1, NF):
-        pl.semaphore_signal(barrier, inc=1, device_id=dev(ff=(feat + d) % NF), device_id_type=MESH)
-    for d in range(1, NZ):
-        pl.semaphore_signal(barrier, inc=1, device_id=dev(zz=(z + d) % NZ), device_id_type=MESH)
-    for d in range(1, NX):
-        pl.semaphore_signal(barrier, inc=1, device_id=dev(xx=(x + d) % NX), device_id_type=MESH)
-    pl.semaphore_signal(barrier, inc=1, device_id=dev(hh=1 - yh), device_id_type=MESH)
 
     first.wait()
     rows = lax.broadcasted_iota(jnp.int32, (PANEL, PANEL), 0)
@@ -103,7 +100,17 @@
         for q in range(Q):
             pan[q, c, y, :, i * part : (i + 1) * part] = turned[q * ROWS : (q + 1) * ROWS, :]
 
-    pl.semaphore_wait(barrier, (NF - 1) + (NZ - 1) + (NX - 1) + 1)
+    rest.wait()
+
+    def add_rows(i, carry):
+        block = abuf[pl.ds(pl.multiple_of(i * 64, 64), 64), :].astype(F32)
+        return carry + jnp.sum(block.reshape(8, 8, width), axis=0)
+
+    sums = lax.fori_loop(0, tokens // 64, add_rows, jnp.zeros((8, width), F32))
+    to_tile(jnp.sum(sums, axis=0, keepdims=True), mf.at[feat])
+
+
+    pl.semaphore_wait(barrier, len(greet))
 
     def panel_copy(q, yy, to, n):
         to = jnp.clip(to, 0, NY - 1)
@@ -113,12 +120,20 @@
     def share_copy(q, yy):
         return remote(pan.at[q, c, yy], pan.at[q, c, yy], ag_s.at[5], ag_pr.at[q], dev(ff=y * NC + 1 - c))
 
-    def ag_own(q):
-        for n, step in enumerate((1, -1, 2, -2)):
-            @pl.when((y + step >= 0) & (y + step < NY))
+    at_end = (y == 0) | (y == NY - 1)
+
+    def send_own(q, steps, extra):
+        for n, step in steps:
+            @pl.when((y + step >= 0) & (y + step < NY) & extra)
             def _():
                 panel_copy(q, y, y + step, n).start()
 
+    def ag_far(q):
+        send_own(q, ((0, 2), (1, -2)), at_end)
+
+    def ag_near(q):
+        send_own(q, ((0, 2), (1, -2)), jnp.logical_not(at_end))
+        send_own(q, ((2, 1), (3, -1)), True)
         share_copy(q, y).start()
 
     def got(q, yy):
@@ -151,7 +166,7 @@
 
     def ag_drain():
         own = pan.at[:, c, y]
-        for n, step in enumerate((1, -1, 2, -2)):
+        for n, step in enumerate((2, -2, 1, -1)):
             @pl.when((y + step >= 0) & (y + step < NY))
             def _():
                 remote(own, own, ag_s.at[n], ag_r.at[0, 0], dev(ff=y * NC + 1 - c)).wait_send()
@@ -174,8 +189,11 @@
     def exchange_wait(buf, own, n, send, recv, where):
         rest_of = buf.at[pl.ds(0, n - 1)]
         every = remote(rest_of, rest_of, send, recv, where((own + 1) % n))
-        every.wait_send()
         every.wait_recv()
+
+    def exchange_sent(buf, n, send, recv, where):
+        rest_of = buf.at[pl.ds(0, n - 1)]
+        remote(rest_of, rest_of, send, recv, where(0)).wait_send()
 
     def at_z(to):
         return dev(zz=to)
@@ -217,7 +235,17 @@
                 xs[q, xx, :, at] = slab.astype(BF16)
             return carry
 
-        lax.fori_loop(0, width // 256, columns, 0)
+        if q < Q - 1:
+            lax.fori_loop(0, width // 256, columns, 0)
+        else:
+            lax.fori_loop(0, width // 512, columns, 0)
+            x_copy(q, 0).start()
+            x_copy(q, 3).start()
+            lax.fori_loop(width // 512, width // 256, columns, 0)
+            x_copy(q, 1).start()
+            x_copy(q, 2).start()
+
+    def xstart(q):
         for m in range(4):
             x_copy(q, m).start()
 
@@ -273,32 +301,38 @@
             ysend[n] = value
             y_send(n).start()
 
-    for q in range(4):
-        ag_own(q)
-    rest.wait()
-
-    def add_rows(i, carry):
-        block = abuf[pl.ds(pl.multiple_of(i * 64, 64), 64), :].astype(F32)
-        return carry + jnp.sum(block.reshape(8, 8, width), axis=0)
-
-    sums = lax.fori_loop(0, tokens // 64, add_rows, jnp.zeros((8, width), F32))
-    to_tile(jnp.sum(sums, axis=0, keepdims=True), mz.at[z])
-
-
+    exchange_start(mf, feat, NF, mf_s, mf_r, at_f)
+    ag_far(0)
+    ag_near(0)
+    ag_far(1)
+    ag_near(1)
+    ag_far(2)
+    mz[z, :8, :] = mf[feat]
+    exchange_wait(mf, feat, NF, mf_s, mf_r, at_f)
+    for f in range(NF):
+        mz[z, 8 + f : 9 + f, :] = mf[f, 0:1, :]
     exchange_start(mz, z, NZ, mz_s, mz_r, at_z)
+    ag_near(2)
+    ag_far(3)
+    ag_near(3)
     exchange_wait(mz, z, NZ, mz_s, mz_r, at_z)
     mx[x] = slot_sum(mz, NZ)
     exchange_start(mx, x, NX, mx_s, mx_r, at_x)
     forward(0)
+    forward(1)
+    ag_far(4)
+    ag_far(5)
     exchange_wait(mx, x, NX, mx_s, mx_r, at_x)
     my[yh] = slot_sum(mx, NX)
     exchange_start(my, yh, NYH, my_s, my_r, at_h)
-    ag_own(4)
-    forward(1)
+    forward(2)
+    forward(3)
+    ag_near(4)
+    ag_far(6)
+    ag_far(7)
+    share(0)
     exchange_wait(my, yh, NYH, my_s, my_r, at_h)
     mean = slot_sum(my, NYH) / total
-    mf[feat] = mean
-    exchange_start(mf, feat, NF, mf_s, mf_r, at_f)
     for i in range(8):
         mrow[:, 128 * i : 128 * (i + 1)] = mean[i : i + 1, :]
 
@@ -308,25 +342,31 @@
         return carry
 
     lax.fori_loop(0, tokens // 64, center, 0)
-    ag_own(5)
-    forward(2)
-    forward(3)
-
-    exchange_wait(mf, feat, NF, mf_s, mf_r, at_f)
+    forward(4)
+    forward(5)
+    ag_near(5)
     for f in range(NF):
-        value = jnp.where(pick, mf[f, 0:1, :], 0.0)
+        value = jnp.where(pick, mean[8 + f : 9 + f, :], 0.0)
         mcol[f] = jnp.broadcast_to(jnp.sum(value, axis=1, keepdims=True), (PANEL, PANEL))
 
-    ag_own(6)
-    forward(4)
-    share(0)
     share(1)
-    ag_own(7)
     compute(0)
-    forward(5)
+    xstart(0)
+    forward(6)
+    ag_near(6)
+    ag_near(7)
     share(2)
     compute(1)
-
+    xstart(1)
+    share(3)
+    compute(2)
+    xphase(0)
+    xstart(2)
+    forward(7)
+    share(4)
+    compute(3)
+    xphase(1)
+    xstart(3)
     tags.wait()
     classes = lax.broadcasted_iota(jnp.int32, (16, tokens), 0)
     onehot = jnp.where(classes == labels_ref[...], 1.0, 0.0).astype(BF16)
@@ -345,58 +385,60 @@
         to = (z + d) % NZ
         remote(crs.at[to], crr.at[z], cr_s, cr_r, at_z(to)).start()
 
-    forward(6)
-    share(3)
-    compute(2)
-    xphase(0)
-    share(4)
-    compute(3)
-    xphase(1)
-    forward(7)
+    share(5)
+    compute(4)
+    xphase(2)
+    xstart(4)
     zphase(0)
+    compute(5)
+    xphase(3)
+    xstart(5)
+    zphase(1)
     exchange_wait(crr, z, NZ, cr_s, cr_r, at_z)
     cx[x] = slot_sum(crr, NZ)
     exchange_start(cx, x, NX, cx_s, cx_r, at_x)
-    share(5)
-    compute(4)
-    xphase(2)
-    zphase(1)
+    share(6)
+    compute(6)
+    xphase(4)
+    xstart(6)
+    zphase(2)
+    zphase(3)
+    xphase(5)
     exchange_wait(cx, x, NX, cx_s, cx_r, at_x)
     cy[yh] = slot_sum(cx, NX)
     exchange_start(cy, yh, NYH, cy_s, cy_r, at_h)
-    share(6)
-    compute(5)
-    xphase(3)
-    zphase(2)
+    share(7)
+    compute(7)
+    xphase(6)
+    zphase(4)
+    zphase(5)
+    yphase(0)
+    yphase(1)
+    xphase(7)
+    zphase(6)
+    yphase(2)
+    yphase(3)
     exchange_wait(cy, yh, NYH, cy_s, cy_r, at_h)
     cg[z] = slot_sum(cy, NYH)
     exchange_start(cg, z, NZ, cg_s, cg_r, at_z)
-    share(7)
-    compute(6)
-    xphase(4)
-    zphase(3)
-    xphase(5)
-    compute(7)
-    zphase(4)
-    xphase(6)
-    zphase(5)
-    xphase(7)
-    zphase(6)
-    yphase(0)
-    yphase(1)
-    yphase(2)
-    yphase(3)
+    zphase(7)
     yphase(4)
+    yphase(5)
+    yphase(6)
+    yphase(7)
     exchange_wait(cg, z, NZ, cg_s, cg_r, at_z)
     for k in range(CLASSES):
         for i in range(8):
             cross_ref[k : k + 1, 128 * i : 128 * (i + 1)] = cg[k, i : i + 1, :] / total
-    zphase(7)
-    yphase(5)
-    yphase(6)
-    yphase(7)
-
     ag_drain()
+    exchange_sent(mf, NF, mf_s, mf_r, at_f)
+    exchange_sent(mz, NZ, mz_s, mz_r, at_z)
+    exchange_sent(mx, NX, mx_s, mx_r, at_x)
+    exchange_sent(my, NYH, my_s, my_r, at_h)
+    exchange_sent(crr, NZ, cr_s, cr_r, at_z)
+    exchange_sent(cx, NX, cx_s, cx_r, at_x)
+    exchange_sent(cy, NYH, cy_s, cy_r, at_h)
+    exchange_sent(cg, NZ, cg_s, cg_r, at_z)
     for m in range(6):
         sent = xr.at[:, m]
         remote(sent, sent, x_s.at[m], x_r.at[0, 0], dev(xx=right)).wait_send()
@@ -429,9 +471,9 @@
         vm((Q // 2, 16, width // 4), F32),
         vm((Q // 2, 16, width // 4), F32),
         vm((Q // 2, 16, width // 4), F32),
-        vm((NZ, *tile), F32),
-        vm((NX, *tile), F32),
-        vm((NYH, *tile), F32),
+        vm((NZ, 16, 128), F32),
+        vm((NX, 16, 128), F32),
+        vm((NYH, 16, 128), F32),
         vm((NF, *tile), F32),
         vm((1, width), F32),
         vm((NF, PANEL, PANEL), F32),

time: 84.3 us -> 74.6 us (0.88)
  Pallas kernels: 80.5 us -> 70.2 us
    pallas_call x1, Pallas kernels: 80.5 us -> 70.2 us  [body(): pl.pallas_call(kernel, out_shape=(jax.ShapeDtypeStruct((out_rows, width),...]
where the time goes in v4:
time: 74.6 us; the launch traced here: 73.7 us
  Pallas kernels  70.2 us (94%)
  local copies, waits for them, and re-layouts  2.85 us (4%)
    pallas_call x1, Pallas kernels, body(): pl.pallas_call(kernel, out_shape=(jax.ShapeDtypeStruct((out_rows, width),...  70.2 us
    unnamed x2, local copies, waits for them, and re-layouts  2.85 us

profile of v4, /device:TPU:56, one launch (start us, length us, event | category | flops | bytes accessed | tf_op | source)
XLA Modules:
  0.0 73.7 jit_solution(18312524486483030635)
XLA Ops:
  0.6 70.2 %stats.1 = (f32[16,1024]{1,0:T(8,128)}, f32[8,1024]{1,0:T(8,128)}) custom-call(bf16[2048,1024]{1,0:T(8,128)(2,1)} %act_hbm.1, s32[1,2048]{1,0:T(1,128)} %bitcast.1), custom_call_target="tpu_custom_call" | custom-call | tf_op jit(solution)/shard_map/stats/pallas_call | solution.py:492
  70.9 1.5 %copy.6 = f32[16,1024]{1,0:T(8,128)} copy(f32[16,1024]{1,0:T(8,128)} %get-tuple-element.4) | data formatting | bytes 131072
  72.3 1.4 %copy.7 = f32[8,1024]{1,0:T(8,128)} copy(f32[8,1024]{1,0:T(8,128)} %get-tuple-element.5) | data formatting | bytes 65536

commit v5 on v4

--- a/solution.py
+++ b/solution.py
@@ -394,34 +394,34 @@
     xphase(3)
     xstart(5)
     zphase(1)
-    exchange_wait(crr, z, NZ, cr_s, cr_r, at_z)
-    cx[x] = slot_sum(crr, NZ)
-    exchange_start(cx, x, NX, cx_s, cx_r, at_x)
     share(6)
     compute(6)
     xphase(4)
     xstart(6)
     zphase(2)
+    share(7)
+    exchange_wait(crr, z, NZ, cr_s, cr_r, at_z)
+    cx[x] = slot_sum(crr, NZ)
+    exchange_start(cx, x, NX, cx_s, cx_r, at_x)
+    xphase(5)
     zphase(3)
-    xphase(5)
+    compute(7)
+    xphase(6)
+    zphase(4)
     exchange_wait(cx, x, NX, cx_s, cx_r, at_x)
     cy[yh] = slot_sum(cx, NX)
     exchange_start(cy, yh, NYH, cy_s, cy_r, at_h)
-    share(7)
-    compute(7)
-    xphase(6)
-    zphase(4)
-    zphase(5)
     yphase(0)
     yphase(1)
+    zphase(5)
     xphase(7)
     zphase(6)
     yphase(2)
-    yphase(3)
+    zphase(7)
     exchange_wait(cy, yh, NYH, cy_s, cy_r, at_h)
     cg[z] = slot_sum(cy, NYH)
     exchange_start(cg, z, NZ, cg_s, cg_r, at_z)
-    zphase(7)
+    yphase(3)
     yphase(4)
     yphase(5)
     yphase(6)

time: 74.6 us -> 73.5 us (0.985)
  Pallas kernels: 70.2 us -> 69.3 us
    pallas_call x1, Pallas kernels: 70.2 us -> 69.3 us  [body(): pl.pallas_call(kernel, out_shape=(jax.ShapeDtypeStruct((out_rows, width),...]
where the time goes in v5:
time: 73.5 us; the launch traced here: 72.8 us
  Pallas kernels  69.3 us (94%)
  local copies, waits for them, and re-layouts  2.85 us (4%)
    pallas_call x1, Pallas kernels, body(): pl.pallas_call(kernel, out_shape=(jax.ShapeDtypeStruct((out_rows, width),...  69.3 us
    unnamed x2, local copies, waits for them, and re-layouts  2.85 us

profile of v5, /device:TPU:56, one launch (start us, length us, event | category | flops | bytes accessed | tf_op | source)
XLA Modules:
  0.0 72.8 jit_solution(4715300852585036698)
XLA Ops:
  0.6 69.3 %stats.1 = (f32[16,1024]{1,0:T(8,128)}, f32[8,1024]{1,0:T(8,128)}) custom-call(bf16[2048,1024]{1,0:T(8,128)(2,1)} %act_hbm.1, s32[1,2048]{1,0:T(1,128)} %bitcast.1), custom_call_target="tpu_custom_call" | custom-call | tf_op jit(solution)/shard_map/stats/pallas_call | solution.py:492
  70.0 1.5 %copy.6 = f32[16,1024]{1,0:T(8,128)} copy(f32[16,1024]{1,0:T(8,128)} %get-tuple-element.4) | data formatting | bytes 131072
  71.5 1.4 %copy.7 = f32[8,1024]{1,0:T(8,128)} copy(f32[8,1024]{1,0:T(8,128)} %get-tuple-element.5) | data formatting | bytes 65536

commit v6 on v5

--- a/solution.py
+++ b/solution.py
@@ -41,9 +41,9 @@
 
 
 def kernel(
-    act_hbm, labels_hbm, cov_ref, cross_ref,
+    act_hbm, labels_hbm, cov_out, cross_out,
     abuf, labels_ref, cbuf, pan, lhs, accf, xs, xr, zsum, zs, zr, ykeep, ysend, yr,
-    mz, mx, my, mf, mrow, mcol, crs, crr, cx, cy, cg,
+    mz, mx, my, mf, mrow, mcol, crs, crr, cx, cy, cg, cov_ref, cross_ref, out_sem,
     load_sem, ag_r, ag_pr, ag_s, x_s, x_r, z_s, z_r, y_s, y_r,
     mz_s, mz_r, mx_s, mx_r, my_s, my_r, mf_s, mf_r,
     cr_s, cr_r, cx_s, cx_r, cy_s, cy_r, cg_s, cg_r,
@@ -71,12 +71,6 @@
             device_id=device, device_id_type=MESH,
         )
 
-    barrier = pltpu.get_barrier_semaphore()
-    greet = [dev(zz=(z + d) % NZ) for d in (4, 3, 5, 2, 6, 1, 7)] + [dev(hh=1 - yh)]
-    greet += [dev(ff=(feat + d) % NF) for d in range(1, NF)] + [dev(xx=(x + d) % NX) for d in range(1, NX)]
-    for device in greet:
-        pl.semaphore_signal(barrier, inc=1, device_id=device, device_id_type=MESH)
-
     first = pltpu.make_async_copy(
         act_hbm.at[:, pl.ds(0, PANEL)], abuf.at[:, pl.ds(0, PANEL)], load_sem.at[0])
     rest = pltpu.make_async_copy(
@@ -86,6 +80,12 @@
     first.start()
     rest.start()
     tags.start()
+
+    barrier = pltpu.get_barrier_semaphore()
+    greet = [dev(zz=(z + d) % NZ) for d in (4, 3, 5, 2, 6, 1, 7)] + [dev(hh=1 - yh)]
+    greet += [dev(ff=(feat + d) % NF) for d in range(1, NF)] + [dev(xx=(x + d) % NX) for d in range(1, NX)]
+    for device in greet:
+        pl.semaphore_signal(barrier, inc=1, device_id=device, device_id_type=MESH)
 
     first.wait()
     rows = lax.broadcasted_iota(jnp.int32, (PANEL, PANEL), 0)
@@ -283,7 +283,7 @@
             z_send(q, d).start()
 
     def y_send(n):
-        return remote(ysend.at[n], yr.at[n], y_s, y_r, dev(hh=1 - yh))
+        return remote(ysend.at[n], yr.at[n], y_s, y_r.at[n], dev(hh=1 - yh))
 
     def yphase(q):
         remote(zr.at[q], zr.at[q], z_s, z_r.at[q], dev(zz=(z + 1) % NZ)).wait_recv()
@@ -430,6 +430,20 @@
     for k in range(CLASSES):
         for i in range(8):
             cross_ref[k : k + 1, 128 * i : 128 * (i + 1)] = cg[k, i : i + 1, :] / total
+    cross_copy = pltpu.make_async_copy(cross_ref, cross_out, out_sem.at[2])
+    cross_copy.start()
+    cov_copies = []
+    for n in range(Q // 2):
+        y_send(n).wait_recv()
+        value = (ykeep[n] + yr[n]) / (total - 1)
+        for i in range(4):
+            cov_ref[4 * n : 4 * n + 4, quarter * i : quarter * (i + 1)] = value[4 * i : 4 * i + 4, :]
+        if n % 2:
+            rows = pl.ds(4 * n - 4, 8)
+            copy = pltpu.make_async_copy(cov_ref.at[rows], cov_out.at[rows], out_sem.at[n // 2])
+            copy.start()
+            cov_copies.append(copy)
+
     ag_drain()
     exchange_sent(mf, NF, mf_s, mf_r, at_f)
     exchange_sent(mz, NZ, mz_s, mz_r, at_z)
@@ -443,16 +457,14 @@
         sent = xr.at[:, m]
         remote(sent, sent, x_s.at[m], x_r.at[0, 0], dev(xx=right)).wait_send()
     remote(zr, zr, z_s, z_r.at[0], dev(zz=(z + 1) % NZ)).wait_send()
-    remote(ysend, ysend, y_s, y_r, dev(hh=1 - yh)).wait_send()
-    remote(yr, yr, y_s, y_r, dev(hh=1 - yh)).wait_recv()
-    for n in range(Q // 2):
-        value = (ykeep[n] + yr[n]) / (total - 1)
-        for i in range(4):
-            cov_ref[4 * n : 4 * n + 4, quarter * i : quarter * (i + 1)] = value[4 * i : 4 * i + 4, :]
-
+    remote(ysend, ysend, y_s, y_r.at[0], dev(hh=1 - yh)).wait_send()
+    for copy in cov_copies:
+        copy.wait()
+    cross_copy.wait()
 
 def body(activations, labels):
     tokens, width = activations.shape
+    out_rows = NF * PANEL // (NZ * NYH * NX)
     dma = pltpu.SemaphoreType.DMA
     vm = pltpu.VMEM
     tile = (8, 128)
@@ -482,13 +494,15 @@
         vm((NX, *tile), F32),
         vm((NYH, *tile), F32),
         vm((NZ, *tile), F32),
+        vm((out_rows, width), F32),
+        vm((CLASSES, width), F32),
+        dma((3,)),
         dma((3,)),
         dma((Q, NY)), dma((Q,)), dma((6,)),
         dma((6,)), dma((Q, 3)),
         dma(()), dma((Q,)),
-        dma(()), dma(()),
+        dma(()), dma((Q // 2,)),
     ] + [dma(())] * 16
-    out_rows = NF * PANEL // (NZ * NYH * NX)
     return pl.pallas_call(
         kernel,
         out_shape=(
@@ -500,8 +514,8 @@
             pl.BlockSpec(memory_space=pl.ANY),
         ],
         out_specs=(
-            pl.BlockSpec(memory_space=pltpu.VMEM),
-            pl.BlockSpec(memory_space=pltpu.VMEM),
+            pl.BlockSpec(memory_space=pl.ANY),
+            pl.BlockSpec(memory_space=pl.ANY),
         ),
         scratch_shapes=scratch,
         compiler_params=pltpu.CompilerParams(

time: 73.5 us -> 73.5 us (level)
  no operation moved by 1% of the time
where the time goes in v6:
time: 73.5 us; the launch traced here: 72.8 us
  Pallas kernels  69.3 us (94%)
  local copies, waits for them, and re-layouts  2.85 us (4%)
    pallas_call x1, Pallas kernels, body(): pl.pallas_call(kernel, out_shape=(jax.ShapeDtypeStruct((out_rows, width),...  69.3 us
    unnamed x2, local copies, waits for them, and re-layouts  2.85 us

profile of v6, /device:TPU:56, one launch (start us, length us, event | category | flops | bytes accessed | tf_op | source)
XLA Modules:
  0.0 72.8 jit_solution(8648007643595580648)
XLA Ops:
  0.6 69.3 %stats.1 = (f32[16,1024]{1,0:T(8,128)}, f32[8,1024]{1,0:T(8,128)}) custom-call(bf16[2048,1024]{1,0:T(8,128)(2,1)} %act_hbm.1, s32[1,2048]{1,0:T(1,128)} %bitcast.1), custom_call_target="tpu_custom_call" | custom-call | tf_op jit(solution)/shard_map/stats/pallas_call | solution.py:506
  70.0 1.5 %copy.6 = f32[16,1024]{1,0:T(8,128)} copy(f32[16,1024]{1,0:T(8,128)} %get-tuple-element.4) | data formatting | bytes 131072
  71.5 1.4 %copy.7 = f32[8,1024]{1,0:T(8,128)} copy(f32[8,1024]{1,0:T(8,128)} %get-tuple-element.5) | data formatting | bytes 65536
